TPU v7x, 32 devices: a whole 2x2x4 slice. The times are simulated.
32 devices in a mesh: dp: 2 (over x), fsdp: 8 (over z, y), seq: 2 (over core).
Axes of the slice: x: 2, y: 2, z: 4, core: 2. Of those that a mesh axis runs over, the one named last changes fastest.
Arguments:
- tokens_in: bfloat16 [16, 1040, 1024], P(('dp', 'fsdp'), 'seq'), may hold values from -6 to 6
- key_mask: int32 [16, 1040], P(('dp', 'fsdp')), may hold values from 0 to 1, as said below
- attn_weights: bfloat16 [2, 1024, 4096], P(None, 'fsdp')
- mlp_weights: bfloat16 [2, 1024, 8192], P(None, 'fsdp')
- vectors: bfloat16 [2, 14, 1024], P(None, None, 'fsdp')
- cotangent: bfloat16 [16, 1040, 1024], P(('dp', 'fsdp'), 'seq'), may hold values from -6 to 6
- first_attn: float32 [2, 1024, 4096], P(None, 'fsdp'), may hold values from -40 to 40
- second_attn: float32 [2, 1024, 4096], P(None, 'fsdp'), may hold values from 0.832 to 8.32
- first_mlp: float32 [2, 1024, 8192], P(None, 'fsdp'), may hold values from -40 to 40
- second_mlp: float32 [2, 1024, 8192], P(None, 'fsdp'), may hold values from 0.832 to 8.32
- first_vec: float32 [2, 14, 1024], P(None, None, 'fsdp'), may hold values from -80 to 80
- second_vec: float32 [2, 14, 1024], P(None, None, 'fsdp'), may hold values from 3.328 to 33.28
Outputs:
- tokens_out: float32 [16, 1040, 1024], P(('dp', 'fsdp'), 'seq')
- grad_tokens: float32 [16, 1040, 1024], P(('dp', 'fsdp'), 'seq')
- grad_attn: float32 [2, 1024, 4096], P(None, 'fsdp')
- grad_mlp: float32 [2, 1024, 8192], P(None, 'fsdp')
- grad_vectors: float32 [2, 14, 1024], P(None, None, 'fsdp')
- step_attn: float32 [2, 1024, 4096], P(None, 'fsdp')
- step_mlp: float32 [2, 1024, 8192], P(None, 'fsdp')
- step_vectors: float32 [2, 14, 1024], P(None, None, 'fsdp')
- new_first_attn: float32 [2, 1024, 4096], P(None, 'fsdp')
- new_second_attn: float32 [2, 1024, 4096], P(None, 'fsdp')
- new_first_mlp: float32 [2, 1024, 8192], P(None, 'fsdp')
- new_second_mlp: float32 [2, 1024, 8192], P(None, 'fsdp')
- new_first_vec: float32 [2, 14, 1024], P(None, None, 'fsdp')
- new_second_vec: float32 [2, 14, 1024], P(None, None, 'fsdp')
Inputs may be any that keep to these rules, and one draw needn't show every extreme that they name: `key_mask`: each image's row is 1 on its first slots and 0 on the rest; at least 910 ones and at least one 0 in every row.
All inputs are finite; a program needn't handle non-finite values.
Results may differ from a plain program's by a relative error of at most 0.023.
Values may be sent and summed in bfloat16 or wider, within the bound.
No kernel may reach another device: no remote copies, remote signals or barrier semaphores. Data moves between devices by JAX's collectives and lax.ppermute only.
A program may use at most 320 MiB of HBM per device.

v0:
```python
import jax
import jax.numpy as jnp
from jax import lax
from jax.sharding import PartitionSpec as P

HD = 64
norm_eps = 1e-06
neg_large = -1e30
beta_first = 0.9
beta_second = 0.999
adam_eps = 1e-08
decay_rate = 0.05
rate_matrix = 0.01
rate_vector = 0.05
step_count = 10.0


def layer_norm(values, norm_gain, norm_shift):
    center = values - jnp.mean(values, axis=-1, keepdims=True)
    spread = jnp.mean(center * center, axis=-1, keepdims=True)
    return center * lax.rsqrt(spread + norm_eps) * norm_gain + norm_shift


def gelu_exact(values):
    return jax.nn.gelu(values, approximate=False)


def contract_last(left_side, right_side):
    return lax.dot_general(
        left_side,
        right_side,
        (((left_side.ndim - 1,), (1,)), ((), ())),
        preferred_element_type=jnp.float32,
    )


def contract_rows(left_side, right_side):
    return lax.dot_general(
        left_side, right_side, (((0, 1), (0, 1)), ((), ())), preferred_element_type=jnp.float32
    )


def masked_scores(query_rows, key_rows, valid_keys):
    scores = contract_last(query_rows, key_rows) * query_rows.shape[-1] ** (-0.5)
    return jnp.where(valid_keys[None, :] > 0, scores, neg_large)


def attend_item(item_set):
    query_rows, key_rows, value_rows, valid_keys = item_set
    scores = masked_scores(query_rows, key_rows, valid_keys)
    row_top = jnp.max(scores, axis=-1, keepdims=True)
    exp_terms = jnp.exp(scores - row_top)
    row_total = jnp.sum(exp_terms, axis=-1, keepdims=True)
    attention = (exp_terms / row_total).astype(jnp.bfloat16)
    mixed_rows = jnp.dot(attention, value_rows, preferred_element_type=jnp.float32)
    return (mixed_rows.astype(jnp.bfloat16), row_top[:, 0] + jnp.log(row_total[:, 0]))


def attend_back(item_set):
    query_rows, key_rows, value_rows, valid_keys, log_total, grad_rows = item_set
    score_scale = query_rows.shape[-1] ** (-0.5)
    scores = masked_scores(query_rows, key_rows, valid_keys)
    attention = jnp.exp(scores - log_total[:, None])
    grad_value = lax.dot_general(
        attention.astype(jnp.bfloat16),
        grad_rows,
        (((0,), (0,)), ((), ())),
        preferred_element_type=jnp.float32,
    )
    grad_attention = contract_last(grad_rows, value_rows)
    inner_sum = jnp.sum(attention * grad_attention, axis=-1, keepdims=True)
    grad_scores = (attention * (grad_attention - inner_sum)).astype(jnp.bfloat16)
    grad_query = jnp.dot(grad_scores, key_rows, preferred_element_type=jnp.float32) * score_scale
    grad_key = (
        lax.dot_general(
            grad_scores, query_rows, (((0,), (0,)), ((), ())), preferred_element_type=jnp.float32
        )
        * score_scale
    )
    return jnp.stack([grad_query, grad_key, grad_value]).astype(jnp.bfloat16)


def forward_layer(inputs, mask_heads, attn_full, mlp_full, vectors_full):
    model_width = attn_full.shape[0]
    hidden = mlp_full.shape[1] // 2
    vec_rows = vectors_full.astype(jnp.float32)
    n_seq = lax.axis_size("seq")
    images, token_rows, _ = inputs.shape
    length = token_rows * n_seq
    group_width = model_width // n_seq
    per_group = group_width // HD
    normed = layer_norm(inputs, vec_rows[0], vec_rows[1]).astype(jnp.bfloat16)
    bias_qkv = jnp.concatenate([vec_rows[2], jnp.zeros_like(vec_rows[2]), vec_rows[3]])
    qkv = (
        jnp.dot(normed, attn_full[:, : 3 * model_width], preferred_element_type=jnp.float32)
        + bias_qkv
    ).astype(jnp.bfloat16)
    heads = lax.all_to_all(
        qkv.reshape(images, token_rows, 3, n_seq, group_width),
        "seq",
        split_axis=3,
        concat_axis=1,
        tiled=True,
    )
    stacked = (
        heads.reshape(images, length, 3, per_group, HD)
        .transpose(2, 0, 3, 1, 4)
        .reshape(3, images * per_group, length, HD)
    )
    mixed_items, log_total = lax.map(attend_item, (stacked[0], stacked[1], stacked[2], mask_heads))
    mixed_heads = (
        mixed_items.reshape(images, per_group, length, HD)
        .transpose(0, 2, 1, 3)
        .reshape(images, length, 1, group_width)
    )
    mixed_rows = lax.all_to_all(
        mixed_heads, "seq", split_axis=1, concat_axis=2, tiled=True
    ).reshape(images, token_rows, model_width)
    branch = contract_last(mixed_rows, attn_full[:, 3 * model_width :]) + vec_rows[4]
    middle = inputs + vec_rows[5] * branch
    normed_two = layer_norm(middle, vec_rows[6], vec_rows[7]).astype(jnp.bfloat16)
    pre_act = jnp.dot(
        normed_two, mlp_full[:, :hidden], preferred_element_type=jnp.float32
    ) + vec_rows[10:].reshape(hidden)
    active = gelu_exact(pre_act).astype(jnp.bfloat16)
    mlp_out = contract_last(active, mlp_full[:, hidden:]) + vec_rows[8]
    output = middle + vec_rows[9] * mlp_out
    saved_set = (
        inputs,
        normed,
        stacked,
        log_total,
        mixed_rows,
        branch,
        middle,
        normed_two,
        pre_act,
        active,
        mlp_out,
    )
    return (output, saved_set)


def backward_layer(upstream, saved_set, attn_full, mlp_full, vectors_full, mask_heads):
    (
        inputs,
        normed,
        stacked,
        log_total,
        mixed_rows,
        branch,
        middle,
        normed_two,
        pre_act,
        active,
        mlp_out,
    ) = saved_set
    model_width = attn_full.shape[0]
    hidden = mlp_full.shape[1] // 2
    vec_rows = vectors_full.astype(jnp.float32)
    n_seq = lax.axis_size("seq")
    images, token_rows, _ = upstream.shape
    length = token_rows * n_seq
    group_width = model_width // n_seq
    per_group = group_width // HD
    grad_scale_two = jnp.sum(upstream * mlp_out, axis=(0, 1))
    grad_mlp_out = (upstream * vec_rows[9]).astype(jnp.bfloat16)
    grad_bias_down = jnp.sum(grad_mlp_out.astype(jnp.float32), axis=(0, 1))
    grad_down = contract_rows(grad_mlp_out, active)
    grad_active = jnp.dot(grad_mlp_out, mlp_full[:, hidden:], preferred_element_type=jnp.float32)
    _, gelu_pull = jax.vjp(gelu_exact, pre_act)
    grad_pre = gelu_pull(grad_active)[0].astype(jnp.bfloat16)
    grad_bias_up = jnp.sum(grad_pre.astype(jnp.float32), axis=(0, 1))
    grad_up = contract_rows(normed_two, grad_pre)
    grad_normed_two = contract_last(grad_pre, mlp_full[:, :hidden])
    _, second_pull = jax.vjp(layer_norm, middle, vec_rows[6], vec_rows[7])
    grad_mid_norm, grad_gain_two, grad_shift_two = second_pull(grad_normed_two)
    grad_middle = upstream + grad_mid_norm
    grad_scale_one = jnp.sum(grad_middle * branch, axis=(0, 1))
    grad_branch = (grad_middle * vec_rows[5]).astype(jnp.bfloat16)
    grad_bias_proj = jnp.sum(grad_branch.astype(jnp.float32), axis=(0, 1))
    grad_proj = contract_rows(grad_branch, mixed_rows)
    grad_mixed = jnp.dot(
        grad_branch, attn_full[:, 3 * model_width :], preferred_element_type=jnp.float32
    ).astype(jnp.bfloat16)
    grad_heads = lax.all_to_all(
        grad_mixed.reshape(images, token_rows, n_seq, group_width),
        "seq",
        split_axis=2,
        concat_axis=1,
        tiled=True,
    )
    grad_items = (
        grad_heads.reshape(images, length, per_group, HD)
        .transpose(0, 2, 1, 3)
        .reshape(images * per_group, length, HD)
    )
    grad_stack = lax.map(
        attend_back, (stacked[0], stacked[1], stacked[2], mask_heads, log_total, grad_items)
    )
    grad_stack = (
        grad_stack.reshape(images, per_group, 3, length, HD)
        .transpose(0, 3, 2, 1, 4)
        .reshape(images, length, 3, 1, group_width)
    )
    grad_qkv = lax.all_to_all(grad_stack, "seq", split_axis=1, concat_axis=3, tiled=True).reshape(
        images, token_rows, 3 * model_width
    )
    grad_qkv_sum = jnp.sum(grad_qkv.astype(jnp.float32), axis=(0, 1))
    grad_qkv_weight = contract_rows(normed, grad_qkv)
    grad_normed = contract_last(grad_qkv, attn_full[:, : 3 * model_width])
    _, first_pull = jax.vjp(layer_norm, inputs, vec_rows[0], vec_rows[1])
    grad_in_norm, grad_gain_one, grad_shift_one = first_pull(grad_normed)
    grad_inputs = grad_middle + grad_in_norm
    grad_attn = jnp.concatenate([grad_qkv_weight, grad_proj], axis=1)
    grad_mlp = jnp.concatenate([grad_up, grad_down], axis=1)
    grad_rows = jnp.stack(
        [
            grad_gain_one,
            grad_shift_one,
            grad_qkv_sum[:model_width],
            grad_qkv_sum[2 * model_width :],
            grad_bias_proj,
            grad_scale_one,
            grad_gain_two,
            grad_shift_two,
            grad_bias_down,
            grad_scale_two,
        ]
    )
    grad_vec = jnp.concatenate(
        [grad_rows, grad_bias_up.reshape(hidden // model_width, model_width)], axis=0
    )
    return (grad_inputs, (grad_attn, grad_mlp, grad_vec))


def adam_step(weights, gradient, moment_one, moment_two, step_rate, decay_weight):
    one_new = beta_first * moment_one + (1.0 - beta_first) * gradient
    two_new = beta_second * moment_two + (1.0 - beta_second) * gradient * gradient
    one_hat = one_new / (1.0 - beta_first**step_count)
    two_hat = two_new / (1.0 - beta_second**step_count)
    change = -step_rate * (
        one_hat / (jnp.sqrt(two_hat) + adam_eps) + decay_weight * weights.astype(jnp.float32)
    )
    return (change, one_new, two_new)


def local(
    tokens_in,
    key_mask,
    attn_weights,
    mlp_weights,
    vectors,
    cotangent,
    first_attn,
    second_attn,
    first_mlp,
    second_mlp,
    first_vec,
    second_vec,
):
    layers = attn_weights.shape[0]
    n_seq = lax.axis_size("seq")
    per_group = attn_weights.shape[2] // 4 // n_seq // HD
    mask_heads = jnp.repeat(key_mask, per_group, axis=0)
    residual = tokens_in.astype(jnp.float32)
    stored = []
    gathered_sets = []
    for layer_index in range(layers):
        weight_set = (
            lax.all_gather(attn_weights[layer_index], "fsdp", axis=0, tiled=True),
            lax.all_gather(mlp_weights[layer_index], "fsdp", axis=0, tiled=True),
            lax.all_gather(vectors[layer_index], "fsdp", axis=1, tiled=True),
        )
        residual, saved_set = forward_layer(
            residual, mask_heads, weight_set[0], weight_set[1], weight_set[2]
        )
        stored.append(saved_set)
        gathered_sets.append(weight_set)
    upstream = cotangent.astype(jnp.float32)
    layer_grads = [None] * layers
    for layer_index in reversed(range(layers)):
        weight_set = (
            lax.all_gather(attn_weights[layer_index], "fsdp", axis=0, tiled=True),
            lax.all_gather(mlp_weights[layer_index], "fsdp", axis=0, tiled=True),
            lax.all_gather(vectors[layer_index], "fsdp", axis=1, tiled=True),
        )
        upstream, local_grads = backward_layer(
            upstream, stored[layer_index], weight_set[0], weight_set[1], weight_set[2], mask_heads
        )
        owned = (
            lax.psum_scatter(
                local_grads[0].astype(jnp.bfloat16), "fsdp", scatter_dimension=0, tiled=True
            ).astype(jnp.float32),
            lax.psum_scatter(
                local_grads[1].astype(jnp.bfloat16), "fsdp", scatter_dimension=0, tiled=True
            ).astype(jnp.float32),
            lax.psum_scatter(
                local_grads[2].astype(jnp.bfloat16), "fsdp", scatter_dimension=1, tiled=True
            ).astype(jnp.float32),
        )
        owned = (
            lax.psum(owned[0].astype(jnp.bfloat16), ("dp", "seq")).astype(jnp.float32),
            lax.psum(owned[1].astype(jnp.bfloat16), ("dp", "seq")).astype(jnp.float32),
            lax.psum(owned[2].astype(jnp.bfloat16), ("dp", "seq")).astype(jnp.float32),
        )
        layer_grads[layer_index] = owned
    grad_attn = jnp.stack([layer_grads[index_one][0] for index_one in range(layers)])
    grad_mlp = jnp.stack([layer_grads[index_one][1] for index_one in range(layers)])
    grad_vectors = jnp.stack([layer_grads[index_one][2] for index_one in range(layers)])
    step_attn, one_attn, two_attn = adam_step(
        attn_weights, grad_attn, first_attn, second_attn, rate_matrix, decay_rate
    )
    step_mlp, one_mlp, two_mlp = adam_step(
        mlp_weights, grad_mlp, first_mlp, second_mlp, rate_matrix, decay_rate
    )
    step_vectors, one_vec, two_vec = adam_step(
        vectors, grad_vectors, first_vec, second_vec, rate_vector, 0.0
    )
    return (
        residual,
        upstream,
        grad_attn,
        grad_mlp,
        grad_vectors,
        step_attn,
        step_mlp,
        step_vectors,
        one_attn,
        two_attn,
        one_mlp,
        two_mlp,
        one_vec,
        two_vec,
    )


def solution(mesh):
    return jax.shard_map(
        local,
        mesh=mesh,
        in_specs=(
            P(("dp", "fsdp"), "seq", None),
            P(("dp", "fsdp"), None),
            P(None, "fsdp", None),
            P(None, "fsdp", None),
            P(None, None, "fsdp"),
            P(("dp", "fsdp"), "seq", None),
            P(None, "fsdp", None),
            P(None, "fsdp", None),
            P(None, "fsdp", None),
            P(None, "fsdp", None),
            P(None, None, "fsdp"),
            P(None, None, "fsdp"),
        ),
        out_specs=(
            P(("dp", "fsdp"), "seq", None),
            P(("dp", "fsdp"), "seq", None),
            P(None, "fsdp", None),
            P(None, "fsdp", None),
            P(None, None, "fsdp"),
            P(None, "fsdp", None),
            P(None, "fsdp", None),
            P(None, None, "fsdp"),
            P(None, "fsdp", None),
            P(None, "fsdp", None),
            P(None, "fsdp", None),
            P(None, "fsdp", None),
            P(None, None, "fsdp"),
            P(None, None, "fsdp"),
        ),
        check_vma=False,
    )
```

profile of v0, /device:TPU:0, one launch (start us, length us, event | category | flops | bytes accessed | tf_op | source)
XLA Modules:
  0.0 2304.5 jit_solution(1958127319763447503)
XLA Ops:
  16.5 23.2 %all-gather = bf16[1,14,1024]{2,0,1:T(2,128)(2,1)S(1)} all-gather(bf16[1,14,128]{2,0,1:T(2,128)(2,1)S(1)} %get-tuple-element.468), channel_id=2, replica_groups=mesh['dp'=2,'fsdp'=8,'seq'=2] {'fsdp'}, dimensions={2}, use_global_device_ids=true | all-gather | bytes 32256 | tf_op jit(solution)/shard_map/all_gather | solution.py:273
  39.9 17.4 all-gather.3
  59.9 79.7 %all-gather.11.cloned.1.call-done = bf16[1,1024,4096]{2,1,0:T(8,128)(2,1)} async-done(((bf16[1,128,4096]{2,1,0:T(8,128)(2,1)}), bf16[1,1024,4096]{2,1,0:T(8,128)(2,1)}) %all-gather.11.cloned.1.call-update) | async-done | bytes 8388624 | tf_op jit(solution)/shard_map/all_gather | solution.py:271
  139.5 8.1 add_convert_fusion.3
  147.6 8.5 reshape.862
  158.6 7.5 all_to_all.120
  166.1 10.3 copy.103
  176.4 8.6 reshape.863
  198.8 72.4 %while.44 = (s32[]{:T(128)}, bf16[8,1040,64]{1,2,0:T(8,128)(2,1)}, f32[8,1040]{1,0:T(8,128)S(1)}, s32[8,1040]{1,0:T(8,128)S(1)}, bf16[8,1040,64]{2,1,0:T(8,128)(...) while((s32[]{:T(128)}, bf16[8,1040,64]{1,2,0:T(8,128)(2,1)}, ...), condition=%wide.region_5.6_spmd, body=%wide.region_2.5_spmd.sunk | while | flops 285608960 | bytes 31756240 | solution.py:110
  271.2 6.4 copy.107
  278.2 8.9 reduce.63
  289.4 7.1 all_to_all.121
  299.9 4.7 fusion.226
  305.0 63.0 %all-gather.13.cloned.1.call-done = bf16[1,1024,8192]{2,1,0:T(8,128)(2,1)} async-done(((bf16[1,128,8192]{2,1,0:T(8,128)(2,1)}), bf16[1,1024,8192]{2,1,0:T(8,128)(2,1)}) %all-gather.13.cloned.1.call-update) | async-done | bytes 16777232 | tf_op jit(solution)/shard_map/all_gather | solution.py:272
  368.1 27.1 %multiply_convert_fusion.3 = (bf16[520,4096]{1,0:T(8,128)(2,1)S(1)}, f32[520,4096]{1,0:T(8,128)}, f32[520,4096]{1,0:T(8,128)}) fusion(f32[4096]{0:T(1024)S(1)} %bitcast.487, bf16[1024,8192]{1,0:T(8,128)(2,1)} %bitcast.522, f32[1,520,1024]{2,1,0:T(8,128)S(1)} %get-tuple-element.424, f32[1024]{0:T(1024)S(1)} %bitcast.513, f32[1024]{0:T(1024)S(1)} %bitcast.499, ...), kind=kOutput, calls=%fused_computation.138 | convolution fusion | flops 4505313280 | bytes 31846464 | tf_op jit(solution)/shard_map/dot_general | solution.py:122
  395.3 11.5 fusion.224
  407.2 86.7 %all-gather.15.cloned.1.call-done = bf16[1,1024,4096]{2,1,0:T(8,128)(2,1)} async-done(((bf16[1,128,4096]{2,1,0:T(8,128)(2,1)}), bf16[1,1024,4096]{2,1,0:T(8,128)(2,1)}) %all-gather.15.cloned.1.call-update) | async-done | bytes 8388624 | tf_op jit(solution)/shard_map/all_gather | solution.py:271
  493.9 8.0 add_convert_fusion.2
  502.0 8.6 reshape.869
  513.0 7.5 all_to_all.122
  520.5 10.3 copy.110
  530.7 8.6 reshape.870
  552.9 68.8 %while.45 = (s32[]{:T(128)}, bf16[8,1040,64]{1,2,0:T(8,128)(2,1)S(1)}, f32[8,1040]{1,0:T(8,128)S(1)}, s32[8,1040]{1,0:T(8,128)S(1)}, bf16[8,1040,64]{2,1,0:T(8,1...) while((s32[]{:T(128)}, ...), condition=%wide.region_13.14_spmd, body=%wide.region_10.13_spmd.sunk | while | flops 285608960 | bytes 31763296 | solution.py:110
  625.8 8.9 reduce.64
  636.2 5.6 all_to_all.123
  647.8 4.7 fusion.223
  654.4 67.8 %all-gather.17.cloned.1.call-done = bf16[1,1024,8192]{2,1,0:T(8,128)(2,1)} async-done(((bf16[1,128,8192]{2,1,0:T(8,128)(2,1)}), bf16[1,1024,8192]{2,1,0:T(8,128)(2,1)}) %all-gather.17.cloned.1.call-update) | async-done | bytes 16777232 | tf_op jit(solution)/shard_map/all_gather | solution.py:272
  722.3 28.0 %multiply_convert_fusion.2 = (bf16[520,4096]{1,0:T(8,128)(2,1)}, f32[520,4096]{1,0:T(8,128)}, f32[520,4096]{1,0:T(8,128)}) fusion(f32[4096]{0:T(1024)S(1)} %bitcast.489, bf16[1024,8192]{1,0:T(8,128)(2,1)} %bitcast.526, f32[1,520,1024]{2,1,0:T(8,128)} %copy-done.8, f32[1024]{0:T(1024)S(1)} %bitcast.511, f32[1024]{0:T(1024)S(1)} %bitcast.495, ...), kind=kOutput, calls=%fused_computation.125 | convolution fusion | flops 4505313280 | bytes 31846464 | tf_op jit(solution)/shard_map/dot_general | solution.py:122
  750.4 14.5 fusion.234
  764.9 9.6 fusion.153
  792.1 99.1 %while.46 = (s32[]{:T(128)}, bf16[8,3,1040,64]{2,3,1,0:T(8,128)(2,1)S(1)}, s32[8,1040]{1,0:T(8,128)}, bf16[8,1040,64]{2,1,0:T(8,128)(2,1)}, bf16[8,1040,64]{2,1,...) while((s32[]{:T(128)}, ...), condition=%wide.region_20.21_spmd, body=%wide.region_18.20_spmd.sunk | while | flops 703489280 | bytes 35388936 | solution.py:198
  893.3 8.4 copy.123
  901.8 8.7 all_to_all.125
  917.1 8.5 reshape.882
  925.7 7.9 fusion.155
  937.0 14.5 fusion.152
  952.4 14.3 fusion.235
  966.7 10.0 fusion.157
  997.4 99.1 %while.47 = (s32[]{:T(128)}, bf16[8,3,1040,64]{2,3,1,0:T(8,128)(2,1)S(1)}, s32[8,1040]{1,0:T(8,128)}, bf16[8,1040,64]{2,1,0:T(8,128)(2,1)}, bf16[8,1040,64]{2,1,...) while((s32[]{:T(128)}, ...), condition=%wide.region_27.28_spmd, body=%wide.region_25.27_spmd.sunk | while | flops 703489280 | bytes 35388936 | solution.py:198
  1098.7 8.4 copy.133
  1107.1 8.7 all_to_all.127
  1122.4 8.4 reshape.890
  1130.9 9.4 convolution_convert_fusion.5
  1140.3 7.0 pad_maximum_fusion.2
  1147.4 4.9 convolution_convert_fusion.6
  1152.3 7.7 convolution_convert_fusion.4
  1160.1 7.8 pad_maximum_fusion.3
  1167.9 9.1 convolution_convert_fusion.2
  1177.0 9.6 convolution_convert_fusion.3
  1186.6 6.6 pad_maximum_fusion
  1193.9 9.3 convolution_convert_fusion
  1203.3 9.6 convolution_convert_fusion.1
  1212.9 6.6 pad_maximum_fusion.1
  1219.6 6.9 fusion.150
  1237.8 56.8 %reduce-scatter.11.cloned.1.call-done = bf16[128,4096]{1,0:T(8,128)(2,1)} async-done(((bf16[1024,4096]{1,0:T(8,128)(2,1)}), bf16[128,4096]{1,0:T(8,128)(2,1)}) %reduce-scatter.11.cloned.1.call-update) | async-done | bytes 1048592 | tf_op jit(solution)/shard_map/reduce_scatter | solution.py:292
  1294.7 152.5 %reduce-scatter.13.cloned.1.call-done = bf16[128,4096]{1,0:T(8,128)(2,1)} async-done(((bf16[1024,4096]{1,0:T(8,128)(2,1)}), bf16[128,4096]{1,0:T(8,128)(2,1)}) %reduce-scatter.13.cloned.1.call-update) | async-done | bytes 1048592 | tf_op jit(solution)/shard_map/reduce_scatter | solution.py:292
  1447.2 285.6 %reduce-scatter.15.cloned.1.call-done = bf16[128,8192]{1,0:T(8,128)(2,1)} async-done(((bf16[1024,8192]{1,0:T(8,128)(2,1)}), bf16[128,8192]{1,0:T(8,128)(2,1)}) %reduce-scatter.15.cloned.1.call-update) | async-done | bytes 2097168 | tf_op jit(solution)/shard_map/reduce_scatter | solution.py:295
  1732.8 286.1 %reduce-scatter.17.cloned.1.call-done = bf16[128,8192]{1,0:T(8,128)(2,1)} async-done(((bf16[1024,8192]{1,0:T(8,128)(2,1)}), bf16[128,8192]{1,0:T(8,128)(2,1)}) %reduce-scatter.17.cloned.1.call-update) | async-done | bytes 2097168 | tf_op jit(solution)/shard_map/reduce_scatter | solution.py:295
  2022.6 60.4 %reduce-scatter.19.cloned.1.call-done = bf16[128,14]{1,0:T(8,128)(2,1)} async-done(((bf16[1024,14]{1,0:T(8,128)(2,1)}), bf16[128,14]{1,0:T(8,128)(2,1)}) %reduce-scatter.19.cloned.1.call-update) | async-done | bytes 3600
  2083.9 63.2 %reduce-scatter.21.cloned.1.call-done = bf16[128,14]{1,0:T(8,128)(2,1)} async-done(((bf16[1024,14]{1,0:T(8,128)(2,1)}), bf16[128,14]{1,0:T(8,128)(2,1)}) %reduce-scatter.21.cloned.1.call-update) | async-done | bytes 3600
  2147.9 5.8 all-reduce
  2156.2 112.7 %all-reduce.4.cloned.1.call-done = (bf16[1,128,4096]{2,1,0:T(8,128)(2,1)}, bf16[1,128,4096]{2,1,0:T(8,128)(2,1)}, bf16[1,128,8192]{2,1,0:T(8,128)(2,1)}, bf16[1,128,8192]{2,1,0:T(8,128)(2,1)}) async-done(((bf16[1,128,4096]{2,1,0:T(8,128)(2,1)}, bf16[1,128,4096]{2,1,0:T(8,128)(2,1)}, bf16[1,128,8192]{2,1,0:T(8,128)(2,1)}, bf16[1,128,8192]{2,1,0:T(8,128)(2,1)}), (bf16[1,128,4096]{2,1,0:T(8,128)(2,1)}, ...) | async-done | bytes 6291472 | tf_op jit(solution)/shard_map/psum | solution.py:303
  2268.9 19.0 add_multiply_fusion
  2288.0 9.8 add_multiply_fusion.1
  (680 shorter events, 481.9 us)
Async XLA Ops:
  7.2 132.3 %all-gather.11.cloned.1.call-start = ((), (), s32[]{:S(2)}) async-start(), calls=%async_computation.18 | async-start | bytes 9437184 | tf_op jit(solution)/shard_map/all_gather | solution.py:271
  10.3 357.7 %all-gather.13.cloned.1.call-start = ((), (), s32[]{:S(2)}) async-start(), calls=%async_computation.19 | async-start | bytes 18874368 | tf_op jit(solution)/shard_map/all_gather | solution.py:272
  15.1 43.5 %copy-start.16 = (bf16[1,520,1024]{2,1,0:T(8,128)(2,1)S(1)}, bf16[1,520,1024]{2,1,0:T(8,128)(2,1)}, u32[]{:S(2)}) copy-start(bf16[1,520,1024]{2,1,0:T(8,128)(2,1)} %param.20) | copy-start | bytes 3194884
  15.1 44.1 %copy-start.101 = (s32[1,1040]{1,0:T(1,128)S(1)}, s32[1,1040]{1,0:T(1,128)}, u32[]{:S(2)}) copy-start(s32[1,1040]{1,0:T(1,128)} %param.21) | copy-start | bytes 12484
  15.1 478.8 %all-gather.15.cloned.1.call-start = ((), (), s32[]{:S(2)}) async-start(), calls=%async_computation.20 | async-start | bytes 9437184 | tf_op jit(solution)/shard_map/all_gather | solution.py:271
  15.8 706.5 %all-gather.17.cloned.1.call-start = ((), (), s32[]{:S(2)}) async-start(), calls=%async_computation.21 | async-start | bytes 18874368 | tf_op jit(solution)/shard_map/all_gather | solution.py:272
  16.4 1278.3 %reduce-scatter.11.cloned.1.call-start = ((), (), s32[]{:S(2)}) async-start(), calls=%async_computation.14 | async-start | bytes 9437184 | tf_op jit(solution)/shard_map/reduce_scatter | solution.py:292
  39.7 107.9 %copy-start.49 = (f32[1,1,1024]{2,0,1:T(1,128)}, f32[1,1,1024]{2,0,1:T(1,128)S(1)}, u32[]{:S(2)}) copy-start(f32[1,1,1024]{2,0,1:T(1,128)S(1)} %get-tuple-element.463) | copy-start | bytes 12292
  39.8 107.8 %copy-start.106 = (f32[1,1,1024]{2,0,1:T(1,128)}, f32[1,1,1024]{2,0,1:T(1,128)S(1)}, u32[]{:S(2)}) copy-start(f32[1,1,1024]{2,0,1:T(1,128)S(1)} %get-tuple-element.464) | copy-start | bytes 12292
  39.8 260.1 %copy-start.66 = (f32[1,1,1024]{2,0,1:T(1,128)}, f32[1,1,1024]{2,0,1:T(1,128)S(1)}, u32[]{:S(2)}) copy-start(f32[1,1,1024]{2,0,1:T(1,128)S(1)} %get-tuple-element.461) | copy-start | bytes 12292
  39.8 260.1 %copy-start.68 = (f32[1,1,1024]{2,0,1:T(1,128)}, f32[1,1,1024]{2,0,1:T(1,128)S(1)}, u32[]{:S(2)}) copy-start(f32[1,1,1024]{2,0,1:T(1,128)S(1)} %get-tuple-element.462) | copy-start | bytes 12292
  39.8 328.3 %copy-start.77 = (f32[1,1,1024]{2,0,1:T(1,128)}, f32[1,1,1024]{2,0,1:T(1,128)S(1)}, u32[]{:S(2)}) copy-start(f32[1,1,1024]{2,0,1:T(1,128)S(1)} %get-tuple-element.459) | copy-start | bytes 12292
  39.8 328.3 %copy-start.104 = (f32[1,1,1024]{2,0,1:T(1,128)}, f32[1,1,1024]{2,0,1:T(1,128)S(1)}, u32[]{:S(2)}) copy-start(f32[1,1,1024]{2,0,1:T(1,128)S(1)} %get-tuple-element.460) | copy-start | bytes 12292
  39.8 355.4 %copy-start.70 = (f32[1,1,1024]{2,0,1:T(1,128)}, f32[1,1,1024]{2,0,1:T(1,128)S(1)}, u32[]{:S(2)}) copy-start(f32[1,1,1024]{2,0,1:T(1,128)S(1)} %get-tuple-element.457) | copy-start | bytes 12292
  39.8 355.4 %copy-start.110 = (f32[1,1,1024]{2,0,1:T(1,128)}, f32[1,1,1024]{2,0,1:T(1,128)S(1)}, u32[]{:S(2)}) copy-start(f32[1,1,1024]{2,0,1:T(1,128)S(1)} %get-tuple-element.458) | copy-start | bytes 12292
  39.9 328.2 %copy-start.72 = (f32[1,4,1024]{2,0,1:T(1,128)}, f32[1,4,1024]{2,0,1:T(1,128)S(1)}, u32[]{:S(2)}) copy-start(f32[1,4,1024]{2,0,1:T(1,128)S(1)} %slice.263) | copy-start | bytes 49156
  58.7 88.9 %copy-start.42 = (f32[520]{0:T(1024)}, f32[520]{0:T(1024)S(1)}, u32[]{:S(2)}) copy-start(f32[520]{0:T(1024)S(1)} %broadcast_multiply_fusion.3) | copy-start | bytes 6244
  59.2 88.4 %copy-start.51 = (f32[520]{0:T(1024)}, f32[520]{0:T(1024)S(1)}, u32[]{:S(2)}) copy-start(f32[520]{0:T(1024)S(1)} %fusion.149) | copy-start | bytes 6244
  59.2 88.4 %copy-start.44 = (f32[520]{0:T(1024)}, f32[520]{0:T(1024)S(1)}, u32[]{:S(2)}) copy-start(f32[520]{0:T(1024)S(1)} %fusion.199) | copy-start | bytes 6244
  271.2 15.9 copy-start.15
  271.2 15.9 copy-start.40
  304.6 90.6 %copy-start.19 = (f32[1,520,1024]{2,1,0:T(8,128)}, f32[1,520,1024]{2,1,0:T(8,128)S(1)}, u32[]{:S(2)}) copy-start(f32[1,520,1024]{2,1,0:T(8,128)S(1)} %get-tuple-element.424) | copy-start | bytes 6389764
  304.6 90.6 %copy-start.57 = (f32[520]{0:T(1024)}, f32[520]{0:T(1024)S(1)}, u32[]{:S(2)}) copy-start(f32[520]{0:T(1024)S(1)} %broadcast_multiply_fusion.2) | copy-start | bytes 6244
  305.0 90.2 %copy-start.53 = (f32[520]{0:T(1024)}, f32[520]{0:T(1024)S(1)}, u32[]{:S(2)}) copy-start(f32[520]{0:T(1024)S(1)} %multiply_reduce_fusion.4) | copy-start | bytes 6244
  305.0 90.2 %copy-start.84 = (f32[520]{0:T(1024)}, f32[520]{0:T(1024)S(1)}, u32[]{:S(2)}) copy-start(f32[520]{0:T(1024)S(1)} %fusion.200) | copy-start | bytes 6244
  395.2 11.6 copy-start.119
  395.3 98.6 %copy-start.81 = (f32[1,1,1024]{2,0,1:T(1,128)S(1)}, f32[1,1,1024]{2,0,1:T(1,128)}, u32[]{:S(2)}) copy-start(f32[1,1,1024]{2,0,1:T(1,128)} %get-tuple-element.453) | copy-start | bytes 12292
  395.3 98.6 %copy-start.93 = (f32[3072]{0:T(1024)S(1)}, f32[3072]{0:T(1024)}, u32[]{:S(2)}) copy-start(f32[3072]{0:T(1024)} %get-tuple-element.473) | copy-start | bytes 36868
  395.3 98.6 %copy-start.108 = (f32[1,1,1024]{2,0,1:T(1,128)S(1)}, f32[1,1,1024]{2,0,1:T(1,128)}, u32[]{:S(2)}) copy-start(f32[1,1,1024]{2,0,1:T(1,128)} %get-tuple-element.454) | copy-start | bytes 12292
  406.8 240.9 %copy-start.5 = (f32[1,520,1024]{2,1,0:T(8,128)}, f32[1,520,1024]{2,1,0:T(8,128)S(1)}, u32[]{:S(2)}) copy-start(f32[1,520,1024]{2,1,0:T(8,128)S(1)} %get-tuple-element.420) | copy-start | bytes 6389764
  406.8 95.1 %copy-start.59 = (f32[520]{0:T(1024)}, f32[520]{0:T(1024)S(1)}, u32[]{:S(2)}) copy-start(f32[520]{0:T(1024)S(1)} %broadcast_multiply_fusion.1) | copy-start | bytes 6244
  407.2 94.8 %copy-start.55 = (f32[520]{0:T(1024)}, f32[520]{0:T(1024)S(1)}, u32[]{:S(2)}) copy-start(f32[520]{0:T(1024)S(1)} %multiply_reduce_fusion.3) | copy-start | bytes 6244
  407.2 94.7 %copy-start.86 = (f32[520]{0:T(1024)}, f32[520]{0:T(1024)S(1)}, u32[]{:S(2)}) copy-start(f32[520]{0:T(1024)S(1)} %fusion.201) | copy-start | bytes 6244
  621.7 13.1 copy-start.39
  621.7 13.1 copy-start.41
  647.8 74.5 %copy-start.74 = (f32[1,4,1024]{2,0,1:T(1,128)S(1)}, f32[1,4,1024]{2,0,1:T(1,128)}, u32[]{:S(2)}) copy-start(f32[1,4,1024]{2,0,1:T(1,128)} %slice.281) | copy-start | bytes 49156
  647.8 74.5 %copy-start.75 = (f32[1,1,1024]{2,0,1:T(1,128)S(1)}, f32[1,1,1024]{2,0,1:T(1,128)}, u32[]{:S(2)}) copy-start(f32[1,1,1024]{2,0,1:T(1,128)} %get-tuple-element.449) | copy-start | bytes 12292
  647.8 74.5 %copy-start.102 = (f32[1,1,1024]{2,0,1:T(1,128)S(1)}, f32[1,1,1024]{2,0,1:T(1,128)}, u32[]{:S(2)}) copy-start(f32[1,1,1024]{2,0,1:T(1,128)} %get-tuple-element.450) | copy-start | bytes 12292
  652.6 122.0 %copy-start.62 = (f32[520]{0:T(1024)}, f32[520]{0:T(1024)S(1)}, u32[]{:S(2)}) copy-start(f32[520]{0:T(1024)S(1)} %broadcast_multiply_fusion) | copy-start | bytes 6244
  654.4 120.1 %copy-start.89 = (f32[520]{0:T(1024)}, f32[520]{0:T(1024)S(1)}, u32[]{:S(2)}) copy-start(f32[520]{0:T(1024)S(1)} %fusion.202) | copy-start | bytes 6244
  722.3 28.1 %copy-start.34 = (bf16[1,520,1024]{2,1,0:T(8,128)(2,1)S(1)}, bf16[1,520,1024]{2,1,0:T(8,128)(2,1)}, u32[]{:S(2)}) copy-start(bf16[1,520,1024]{2,1,0:T(8,128)(2,1)} %param.25) | copy-start | bytes 3194884
  722.3 28.1 %copy-start.79 = (f32[1,1,1024]{2,0,1:T(1,128)S(1)}, f32[1,1,1024]{2,0,1:T(1,128)}, u32[]{:S(2)}) copy-start(f32[1,1,1024]{2,0,1:T(1,128)} %get-tuple-element.447) | copy-start | bytes 12292
  750.4 14.6 copy-start.9
  937.0 14.5 copy-start.71
  952.4 14.3 copy-start.37
  952.4 14.3 copy-start.20
  952.4 14.3 copy-start.58
  952.4 14.3 copy-start.78
  952.4 14.3 copy-start.85
  966.7 10.1 copy-start.121
  966.7 10.1 copy-start.54
  1147.4 299.8 %reduce-scatter.13.cloned.1.call-start = ((), (), s32[]{:S(2)}) async-start(), calls=%async_computation.15 | async-start | bytes 9437184 | tf_op jit(solution)/shard_map/reduce_scatter | solution.py:292
  1167.9 564.9 %reduce-scatter.15.cloned.1.call-start = ((), (), s32[]{:S(2)}) async-start(), calls=%async_computation.16 | async-start | bytes 18874368 | tf_op jit(solution)/shard_map/reduce_scatter | solution.py:295
  1193.3 825.6 %reduce-scatter.17.cloned.1.call-start = ((), (), s32[]{:S(2)}) async-start(), calls=%async_computation.17 | async-start | bytes 18874368 | tf_op jit(solution)/shard_map/reduce_scatter | solution.py:295
  1219.5 863.6 %reduce-scatter.19.cloned.1.call-start = ((), (), s32[]{:S(2)}) async-start(), calls=%async_computation.22 | async-start | bytes 294912
  1234.0 913.1 %reduce-scatter.21.cloned.1.call-start = ((), (), s32[]{:S(2)}) async-start(), calls=%async_computation.23 | async-start | bytes 294912
  1237.6 781.4 %copy-start.13 = (f32[520,1024]{1,0:T(8,128)S(1)}, f32[520,1024]{1,0:T(8,128)}, u32[]{:S(2)}) copy-start(f32[520,1024]{1,0:T(8,128)} %copy-done.12) | copy-start | bytes 6389764
  1237.6 781.4 %copy-start.18 = (bf16[1,520,1024]{2,1,0:T(8,128)(2,1)S(1)}, bf16[1,520,1024]{2,1,0:T(8,128)(2,1)}, u32[]{:S(2)}) copy-start(bf16[1,520,1024]{2,1,0:T(8,128)(2,1)} %param.20) | copy-start | bytes 3194884
  1237.6 1031.3 %all-reduce.4.cloned.1.call-start = ((), (), s32[]{:S(2)}) async-start(), calls=%async_computation.24 | async-start | bytes 12582912 | tf_op jit(solution)/shard_map/psum | solution.py:303
  2019.0 134.8 %copy-start.47 = (bf16[2,14,128]{2,0,1:T(2,128)(2,1)S(1)}, bf16[2,14,128]{2,0,1:T(2,128)(2,1)}, u32[]{:S(2)}) copy-start(bf16[2,14,128]{2,0,1:T(2,128)(2,1)} %param.24) | copy-start | bytes 21508
  2019.0 134.8 %copy-start.91 = (f32[2,14,128]{2,0,1:T(2,128)S(1)}, f32[2,14,128]{2,0,1:T(2,128)}, u32[]{:S(2)}) copy-start(f32[2,14,128]{2,0,1:T(2,128)} %param.30) | copy-start | bytes 43012
  2019.0 134.8 %copy-start.92 = (f32[2,14,128]{2,0,1:T(2,128)S(1)}, f32[2,14,128]{2,0,1:T(2,128)}, u32[]{:S(2)}) copy-start(f32[2,14,128]{2,0,1:T(2,128)} %param.31) | copy-start | bytes 43012
  2268.9 19.0 copy-start.27
  2268.9 19.1 copy-start.38
  (83 other events, 363.0 us)
Sparse Core Ops, SparseCore 0:
  10.7 128.7 all-gather.10
  142.2 225.7 all-gather.12
  370.8 123.1 all-gather.14
  496.5 225.7 all-gather.16
  1147.5 147.1 reduce-scatter.10
  1299.2 147.9 reduce-scatter.12
  1451.0 281.8 reduce-scatter.14
  1737.1 281.7 reduce-scatter.16
  2022.8 60.2 reduce-scatter.18
  2086.8 60.2 reduce-scatter.20
  2149.7 119.1 all-reduce.3
where the time goes:
time: 2320 us; the launch traced here: 2300 us
  waiting for transfers between devices  1320 us (57%)
  matrix products  486 us (21%)
  local copies, waits for them, and re-layouts  247 us (11%)
  other arithmetic  136 us (6%)
  blocking collectives  101 us (4%)
    reduce_scatter x2, waiting for transfers between devices, local(): lax.psum_scatter(local_grads[1].astype(jnp.bfloat16), 'fsdp', scatter_dim...  572 us
    reduce_scatter x2, waiting for transfers between devices, local(): lax.psum_scatter(local_grads[0].astype(jnp.bfloat16), 'fsdp', scatter_dim...  209 us
    dot_general x56, matrix products, contract_last(): lax.dot_general(left_side, right_side, (((left_side.ndim - 1,), (1,)), ((...  176 us
    all_gather x2, waiting for transfers between devices, local(): lax.all_gather(attn_weights[layer_index], 'fsdp', axis=0, tiled=True)  166 us
    all_gather x2, waiting for transfers between devices, local(): lax.all_gather(mlp_weights[layer_index], 'fsdp', axis=0, tiled=True)  131 us
    unnamed x13, waiting for transfers between devices  125 us
    psum x1, waiting for transfers between devices, local(): lax.psum(owned[0].astype(jnp.bfloat16), ('dp', 'seq')).astype(jnp.float32)  113 us
    dot_general x8, matrix products, contract_rows(): lax.dot_general(left_side, right_side, (((0, 1), (0, 1)), ((), ())), pref...  62.7 us
  transfers between devices with their start and end apart: 11, of which 11 were waited for; matrix products, arithmetic and copies ran while one was open for 17% of the time, Pallas kernels for 0%

commit v1 on v0

--- a/solution.py
+++ b/solution.py
@@ -300,7 +300,9 @@
             ).astype(jnp.float32),
         )
         owned = (
-            lax.psum(owned[0].astype(jnp.bfloat16), ("dp", "seq")).astype(jnp.float32),
+            jnp.sum(lax.all_gather(owned[0].astype(jnp.bfloat16), ("dp", "seq")), axis=0).astype(
+                jnp.float32
+            ),
             lax.psum(owned[1].astype(jnp.bfloat16), ("dp", "seq")).astype(jnp.float32),
             lax.psum(owned[2].astype(jnp.bfloat16), ("dp", "seq")).astype(jnp.float32),
         )

time: 2320 us -> 2340 us (level)
    all_gather x0 -> x2, waiting for transfers between devices: none -> 58.8 us  [local(): lax.all_gather(owned[0].astype(jnp.bfloat16), ('dp', 'seq'))]
    psum x1, waiting for transfers between devices: 113 us -> 74.1 us  [local(): lax.psum(owned[1].astype(jnp.bfloat16), ('dp', 'seq')).astype(jnp.float32)]
    unnamed x13 -> x15, waiting for transfers between devices: 125 us -> 125 us
  transfers between devices with their start and end apart: 11 -> 13, of which waited for: 11 -> 13; matrix products, arithmetic and copies ran while one was open for 17% -> 18% of each run, Pallas kernels for 0% -> 0%
where the time goes in v1:
time: 2340 us; the launch traced here: 2330 us
  waiting for transfers between devices  1340 us (57%)
  matrix products  486 us (21%)
  local copies, waits for them, and re-layouts  247 us (11%)
  other arithmetic  143 us (6%)
  blocking collectives  101 us (4%)
    reduce_scatter x2, waiting for transfers between devices, local(): lax.psum_scatter(local_grads[1].astype(jnp.bfloat16), 'fsdp', scatter_dim...  571 us
    reduce_scatter x2, waiting for transfers between devices, local(): lax.psum_scatter(local_grads[0].astype(jnp.bfloat16), 'fsdp', scatter_dim...  209 us
    dot_general x56, matrix products, contract_last(): lax.dot_general(left_side, right_side, (((left_side.ndim - 1,), (1,)), ((...  176 us
    all_gather x2, waiting for transfers between devices, local(): lax.all_gather(attn_weights[layer_index], 'fsdp', axis=0, tiled=True)  166 us
    all_gather x2, waiting for transfers between devices, local(): lax.all_gather(mlp_weights[layer_index], 'fsdp', axis=0, tiled=True)  131 us
    unnamed x15, waiting for transfers between devices  125 us
    psum x1, waiting for transfers between devices, local(): lax.psum(owned[1].astype(jnp.bfloat16), ('dp', 'seq')).astype(jnp.float32)  74.1 us
    dot_general x8, matrix products, contract_rows(): lax.dot_general(left_side, right_side, (((0, 1), (0, 1)), ((), ())), pref...  62.7 us
  transfers between devices with their start and end apart: 13, of which 13 were waited for; matrix products, arithmetic and copies ran while one was open for 18% of the time, Pallas kernels for 0%

profile of v1, /device:TPU:0, one launch (start us, length us, event | category | flops | bytes accessed | tf_op | source)
XLA Modules:
  0.0 2331.6 jit_solution(16864770279141808231)
XLA Ops:
  16.5 23.2 all-gather
  39.9 17.4 all-gather.3
  59.9 79.7 %all-gather.15.cloned.1.call-done = bf16[1,1024,4096]{2,1,0:T(8,128)(2,1)} async-done(((bf16[1,128,4096]{2,1,0:T(8,128)(2,1)}), bf16[1,1024,4096]{2,1,0:T(8,128)(2,1)}) %all-gather.15.cloned.1.call-update) | async-done | bytes 8388624 | tf_op jit(solution)/shard_map/all_gather | solution.py:271
  139.5 8.1 add_convert_fusion.3
  147.6 8.5 reshape.880
  158.6 7.5 all_to_all.120
  166.1 10.2 copy.103
  176.4 8.6 reshape.881
  198.8 72.5 %while.44 = (s32[]{:T(128)}, bf16[8,1040,64]{1,2,0:T(8,128)(2,1)}, f32[8,1040]{1,0:T(8,128)S(1)}, s32[8,1040]{1,0:T(8,128)S(1)}, bf16[8,1040,64]{2,1,0:T(8,128)(...) while((s32[]{:T(128)}, bf16[8,1040,64]{1,2,0:T(8,128)(2,1)}, ...), condition=%wide.region_5.6_spmd, body=%wide.region_2.5_spmd.sunk | while | flops 285608960 | bytes 31756240 | solution.py:110
  271.3 6.4 copy.107
  278.1 8.9 reduce.65
  289.3 7.1 all_to_all.121
  304.9 63.2 %all-gather.17.cloned.1.call-done = bf16[1,1024,8192]{2,1,0:T(8,128)(2,1)} async-done(((bf16[1,128,8192]{2,1,0:T(8,128)(2,1)}), bf16[1,1024,8192]{2,1,0:T(8,128)(2,1)}) %all-gather.17.cloned.1.call-update) | async-done | bytes 16777232 | tf_op jit(solution)/shard_map/all_gather | solution.py:272
  368.1 27.0 %multiply_convert_fusion.3 = (bf16[520,4096]{1,0:T(8,128)(2,1)S(1)}, f32[520,4096]{1,0:T(8,128)}, f32[520,4096]{1,0:T(8,128)}) fusion(f32[4096]{0:T(1024)S(1)} %bitcast.491, bf16[1024,8192]{1,0:T(8,128)(2,1)} %bitcast.526, f32[1,520,1024]{2,1,0:T(8,128)S(1)} %get-tuple-element.422, f32[1024]{0:T(1024)S(1)} %bitcast.517, f32[1024]{0:T(1024)S(1)} %bitcast.503, ...), kind=kOutput, calls=%fused_computation.138 | convolution fusion | flops 4505313280 | bytes 31846464 | tf_op jit(solution)/shard_map/dot_general | solution.py:122
  395.2 11.5 fusion.224
  407.1 86.8 %all-gather.19.cloned.1.call-done = bf16[1,1024,4096]{2,1,0:T(8,128)(2,1)} async-done(((bf16[1,128,4096]{2,1,0:T(8,128)(2,1)}), bf16[1,1024,4096]{2,1,0:T(8,128)(2,1)}) %all-gather.19.cloned.1.call-update) | async-done | bytes 8388624 | tf_op jit(solution)/shard_map/all_gather | solution.py:271
  493.9 8.0 add_convert_fusion.2
  502.0 8.6 reshape.887
  513.0 7.5 all_to_all.122
  520.5 10.2 copy.110
  530.7 8.6 reshape.888
  552.9 68.8 %while.45 = (s32[]{:T(128)}, bf16[8,1040,64]{1,2,0:T(8,128)(2,1)S(1)}, f32[8,1040]{1,0:T(8,128)S(1)}, s32[8,1040]{1,0:T(8,128)S(1)}, bf16[8,1040,64]{2,1,0:T(8,1...) while((s32[]{:T(128)}, ...), condition=%wide.region_13.14_spmd, body=%wide.region_10.13_spmd.sunk | while | flops 285608960 | bytes 31763296 | solution.py:110
  625.8 8.9 reduce.66
  636.2 5.6 all_to_all.123
  654.3 67.9 %all-gather.21.cloned.1.call-done = bf16[1,1024,8192]{2,1,0:T(8,128)(2,1)} async-done(((bf16[1,128,8192]{2,1,0:T(8,128)(2,1)}), bf16[1,1024,8192]{2,1,0:T(8,128)(2,1)}) %all-gather.21.cloned.1.call-update) | async-done | bytes 16777232 | tf_op jit(solution)/shard_map/all_gather | solution.py:272
  722.3 28.0 %multiply_convert_fusion.2 = (bf16[520,4096]{1,0:T(8,128)(2,1)}, f32[520,4096]{1,0:T(8,128)}, f32[520,4096]{1,0:T(8,128)}) fusion(f32[4096]{0:T(1024)S(1)} %bitcast.493, bf16[1024,8192]{1,0:T(8,128)(2,1)} %bitcast.530, f32[1,520,1024]{2,1,0:T(8,128)} %copy-done.8, f32[1024]{0:T(1024)S(1)} %bitcast.515, f32[1024]{0:T(1024)S(1)} %bitcast.499, ...), kind=kOutput, calls=%fused_computation.125 | convolution fusion | flops 4505313280 | bytes 31846464 | tf_op jit(solution)/shard_map/dot_general | solution.py:122
  750.4 14.5 fusion.234
  764.9 9.6 fusion.153
  792.1 99.1 %while.46 = (s32[]{:T(128)}, bf16[8,3,1040,64]{2,3,1,0:T(8,128)(2,1)S(1)}, s32[8,1040]{1,0:T(8,128)}, bf16[8,1040,64]{2,1,0:T(8,128)(2,1)}, bf16[8,1040,64]{2,1,...) while((s32[]{:T(128)}, ...), condition=%wide.region_20.21_spmd, body=%wide.region_18.20_spmd.sunk | while | flops 703489280 | bytes 35388936 | solution.py:198
  893.4 8.4 copy.123
  901.8 8.7 all_to_all.125
  917.2 8.5 reshape.900
  925.7 7.9 fusion.155
  937.0 14.4 fusion.152
  952.4 14.3 fusion.235
  966.7 10.0 fusion.157
  997.2 99.1 %while.47 = (s32[]{:T(128)}, bf16[8,3,1040,64]{2,3,1,0:T(8,128)(2,1)S(1)}, s32[8,1040]{1,0:T(8,128)}, bf16[8,1040,64]{2,1,0:T(8,128)(2,1)}, bf16[8,1040,64]{2,1,...) while((s32[]{:T(128)}, ...), condition=%wide.region_27.28_spmd, body=%wide.region_25.27_spmd.sunk | while | flops 703489280 | bytes 35388936 | solution.py:198
  1098.5 8.4 copy.133
  1107.0 8.7 all_to_all.127
  1122.3 8.4 reshape.908
  1130.7 9.4 convolution_convert_fusion.5
  1140.2 7.0 pad_maximum_fusion.2
  1147.3 4.9 convolution_convert_fusion.6
  1152.2 7.7 convolution_convert_fusion.4
  1159.9 7.8 pad_maximum_fusion.3
  1167.8 9.1 convolution_convert_fusion.2
  1176.9 9.6 convolution_convert_fusion.3
  1186.5 6.6 pad_maximum_fusion
  1193.8 9.3 convolution_convert_fusion
  1203.1 9.6 convolution_convert_fusion.1
  1212.7 6.6 pad_maximum_fusion.1
  1219.4 6.8 fusion.150
  1237.5 56.9 %reduce-scatter.11.cloned.1.call-done = bf16[128,4096]{1,0:T(8,128)(2,1)} async-done(((bf16[1024,4096]{1,0:T(8,128)(2,1)}), bf16[128,4096]{1,0:T(8,128)(2,1)}) %reduce-scatter.11.cloned.1.call-update) | async-done | bytes 1048592 | tf_op jit(solution)/shard_map/reduce_scatter | solution.py:292
  1294.6 152.3 %reduce-scatter.13.cloned.1.call-done = bf16[128,4096]{1,0:T(8,128)(2,1)} async-done(((bf16[1024,4096]{1,0:T(8,128)(2,1)}), bf16[128,4096]{1,0:T(8,128)(2,1)}) %reduce-scatter.13.cloned.1.call-update) | async-done | bytes 1048592 | tf_op jit(solution)/shard_map/reduce_scatter | solution.py:292
  1447.0 285.4 %reduce-scatter.15.cloned.1.call-done = bf16[128,8192]{1,0:T(8,128)(2,1)} async-done(((bf16[1024,8192]{1,0:T(8,128)(2,1)}), bf16[128,8192]{1,0:T(8,128)(2,1)}) %reduce-scatter.15.cloned.1.call-update) | async-done | bytes 2097168 | tf_op jit(solution)/shard_map/reduce_scatter | solution.py:295
  1732.4 286.0 %reduce-scatter.17.cloned.1.call-done = bf16[128,8192]{1,0:T(8,128)(2,1)} async-done(((bf16[1024,8192]{1,0:T(8,128)(2,1)}), bf16[128,8192]{1,0:T(8,128)(2,1)}) %reduce-scatter.17.cloned.1.call-update) | async-done | bytes 2097168 | tf_op jit(solution)/shard_map/reduce_scatter | solution.py:295
  2022.2 60.6 %reduce-scatter.19.cloned.1.call-done = bf16[128,14]{1,0:T(8,128)(2,1)} async-done(((bf16[1024,14]{1,0:T(8,128)(2,1)}), bf16[128,14]{1,0:T(8,128)(2,1)}) %reduce-scatter.19.cloned.1.call-update) | async-done | bytes 3600
  2083.6 63.3 %reduce-scatter.21.cloned.1.call-done = bf16[128,14]{1,0:T(8,128)(2,1)} async-done(((bf16[1024,14]{1,0:T(8,128)(2,1)}), bf16[128,14]{1,0:T(8,128)(2,1)}) %reduce-scatter.21.cloned.1.call-update) | async-done | bytes 3600
  2147.6 5.8 all-reduce
  2155.9 26.0 %all-gather.23.cloned.1.call-done = bf16[512,4096]{1,0:T(8,128)(2,1)} async-done(((bf16[128,4096]{1,0:T(8,128)(2,1)}), bf16[512,4096]{1,0:T(8,128)(2,1)}) %all-gather.23.cloned.1.call-update) | async-done | bytes 4194320 | tf_op jit(solution)/shard_map/all_gather | solution.py:303
  2185.0 32.9 %all-gather.25.cloned.1.call-done = bf16[512,4096]{1,0:T(8,128)(2,1)} async-done(((bf16[128,4096]{1,0:T(8,128)(2,1)}), bf16[512,4096]{1,0:T(8,128)(2,1)}) %all-gather.25.cloned.1.call-update) | async-done | bytes 4194320 | tf_op jit(solution)/shard_map/all_gather | solution.py:303
  2222.1 9.8 add_multiply_fusion.1
  2231.9 74.1 %all-reduce.4.cloned.1.call-done = (bf16[1,128,8192]{2,1,0:T(8,128)(2,1)}, bf16[1,128,8192]{2,1,0:T(8,128)(2,1)}) async-done(((bf16[1,128,8192]{2,1,0:T(8,128)(2,1)}, bf16[1,128,8192]{2,1,0:T(8,128)(2,1)}), (bf16[1,128,8192]{2,1,0:T(8,128)(2,1)}, bf16[1,128,8192]{2,1,0:T(8,128)(2,1)})) %all-reduce.4.cloned.1.call-update) | async-done | bytes 4194320 | tf_op jit(solution)/shard_map/psum | solution.py:306
  2306.0 18.9 add_multiply_fusion
  (686 shorter events, 498.6 us)
Async XLA Ops:
  7.2 132.3 %all-gather.15.cloned.1.call-start = ((), (), s32[]{:S(2)}) async-start(), calls=%async_computation.18 | async-start | bytes 9437184 | tf_op jit(solution)/shard_map/all_gather | solution.py:271
  10.3 357.7 %all-gather.17.cloned.1.call-start = ((), (), s32[]{:S(2)}) async-start(), calls=%async_computation.19 | async-start | bytes 18874368 | tf_op jit(solution)/shard_map/all_gather | solution.py:272
  15.1 43.5 %copy-start.16 = (bf16[1,520,1024]{2,1,0:T(8,128)(2,1)S(1)}, bf16[1,520,1024]{2,1,0:T(8,128)(2,1)}, u32[]{:S(2)}) copy-start(bf16[1,520,1024]{2,1,0:T(8,128)(2,1)} %param.20) | copy-start | bytes 3194884
  15.1 44.1 %copy-start.100 = (s32[1,1040]{1,0:T(1,128)S(1)}, s32[1,1040]{1,0:T(1,128)}, u32[]{:S(2)}) copy-start(s32[1,1040]{1,0:T(1,128)} %param.21) | copy-start | bytes 12484
  15.1 478.8 %all-gather.19.cloned.1.call-start = ((), (), s32[]{:S(2)}) async-start(), calls=%async_computation.20 | async-start | bytes 9437184 | tf_op jit(solution)/shard_map/all_gather | solution.py:271
  15.8 706.5 %all-gather.21.cloned.1.call-start = ((), (), s32[]{:S(2)}) async-start(), calls=%async_computation.21 | async-start | bytes 18874368 | tf_op jit(solution)/shard_map/all_gather | solution.py:272
  16.4 1278.0 %reduce-scatter.11.cloned.1.call-start = ((), (), s32[]{:S(2)}) async-start(), calls=%async_computation.14 | async-start | bytes 9437184 | tf_op jit(solution)/shard_map/reduce_scatter | solution.py:292
  39.7 107.9 %copy-start.48 = (f32[1,1,1024]{2,0,1:T(1,128)}, f32[1,1,1024]{2,0,1:T(1,128)S(1)}, u32[]{:S(2)}) copy-start(f32[1,1,1024]{2,0,1:T(1,128)S(1)} %get-tuple-element.461) | copy-start | bytes 12292
  39.8 107.8 %copy-start.105 = (f32[1,1,1024]{2,0,1:T(1,128)}, f32[1,1,1024]{2,0,1:T(1,128)S(1)}, u32[]{:S(2)}) copy-start(f32[1,1,1024]{2,0,1:T(1,128)S(1)} %get-tuple-element.462) | copy-start | bytes 12292
  39.8 260.0 %copy-start.65 = (f32[1,1,1024]{2,0,1:T(1,128)}, f32[1,1,1024]{2,0,1:T(1,128)S(1)}, u32[]{:S(2)}) copy-start(f32[1,1,1024]{2,0,1:T(1,128)S(1)} %get-tuple-element.459) | copy-start | bytes 12292
  39.8 260.0 %copy-start.67 = (f32[1,1,1024]{2,0,1:T(1,128)}, f32[1,1,1024]{2,0,1:T(1,128)S(1)}, u32[]{:S(2)}) copy-start(f32[1,1,1024]{2,0,1:T(1,128)S(1)} %get-tuple-element.460) | copy-start | bytes 12292
  39.8 328.3 %copy-start.76 = (f32[1,1,1024]{2,0,1:T(1,128)}, f32[1,1,1024]{2,0,1:T(1,128)S(1)}, u32[]{:S(2)}) copy-start(f32[1,1,1024]{2,0,1:T(1,128)S(1)} %get-tuple-element.457) | copy-start | bytes 12292
  39.8 328.3 %copy-start.103 = (f32[1,1,1024]{2,0,1:T(1,128)}, f32[1,1,1024]{2,0,1:T(1,128)S(1)}, u32[]{:S(2)}) copy-start(f32[1,1,1024]{2,0,1:T(1,128)S(1)} %get-tuple-element.458) | copy-start | bytes 12292
  39.8 355.3 %copy-start.69 = (f32[1,1,1024]{2,0,1:T(1,128)}, f32[1,1,1024]{2,0,1:T(1,128)S(1)}, u32[]{:S(2)}) copy-start(f32[1,1,1024]{2,0,1:T(1,128)S(1)} %get-tuple-element.455) | copy-start | bytes 12292
  39.8 355.3 %copy-start.109 = (f32[1,1,1024]{2,0,1:T(1,128)}, f32[1,1,1024]{2,0,1:T(1,128)S(1)}, u32[]{:S(2)}) copy-start(f32[1,1,1024]{2,0,1:T(1,128)S(1)} %get-tuple-element.456) | copy-start | bytes 12292
  39.9 328.2 %copy-start.71 = (f32[1,4,1024]{2,0,1:T(1,128)}, f32[1,4,1024]{2,0,1:T(1,128)S(1)}, u32[]{:S(2)}) copy-start(f32[1,4,1024]{2,0,1:T(1,128)S(1)} %slice.263) | copy-start | bytes 49156
  58.7 88.9 %copy-start.41 = (f32[520]{0:T(1024)}, f32[520]{0:T(1024)S(1)}, u32[]{:S(2)}) copy-start(f32[520]{0:T(1024)S(1)} %broadcast_multiply_fusion.3) | copy-start | bytes 6244
  59.2 88.4 %copy-start.50 = (f32[520]{0:T(1024)}, f32[520]{0:T(1024)S(1)}, u32[]{:S(2)}) copy-start(f32[520]{0:T(1024)S(1)} %fusion.149) | copy-start | bytes 6244
  59.2 88.4 %copy-start.43 = (f32[520]{0:T(1024)}, f32[520]{0:T(1024)S(1)}, u32[]{:S(2)}) copy-start(f32[520]{0:T(1024)S(1)} %fusion.199) | copy-start | bytes 6244
  271.3 15.8 copy-start.15
  271.3 15.8 copy-start.39
  304.5 90.6 %copy-start.19 = (f32[1,520,1024]{2,1,0:T(8,128)}, f32[1,520,1024]{2,1,0:T(8,128)S(1)}, u32[]{:S(2)}) copy-start(f32[1,520,1024]{2,1,0:T(8,128)S(1)} %get-tuple-element.422) | copy-start | bytes 6389764
  304.5 90.6 %copy-start.56 = (f32[520]{0:T(1024)}, f32[520]{0:T(1024)S(1)}, u32[]{:S(2)}) copy-start(f32[520]{0:T(1024)S(1)} %broadcast_multiply_fusion.2) | copy-start | bytes 6244
  304.9 90.3 %copy-start.52 = (f32[520]{0:T(1024)}, f32[520]{0:T(1024)S(1)}, u32[]{:S(2)}) copy-start(f32[520]{0:T(1024)S(1)} %multiply_reduce_fusion.4) | copy-start | bytes 6244
  304.9 90.3 %copy-start.83 = (f32[520]{0:T(1024)}, f32[520]{0:T(1024)S(1)}, u32[]{:S(2)}) copy-start(f32[520]{0:T(1024)S(1)} %fusion.200) | copy-start | bytes 6244
  395.1 11.6 copy-start.118
  395.2 98.7 %copy-start.80 = (f32[1,1,1024]{2,0,1:T(1,128)S(1)}, f32[1,1,1024]{2,0,1:T(1,128)}, u32[]{:S(2)}) copy-start(f32[1,1,1024]{2,0,1:T(1,128)} %get-tuple-element.451) | copy-start | bytes 12292
  395.2 98.7 %copy-start.92 = (f32[3072]{0:T(1024)S(1)}, f32[3072]{0:T(1024)}, u32[]{:S(2)}) copy-start(f32[3072]{0:T(1024)} %get-tuple-element.471) | copy-start | bytes 36868
  395.2 98.7 %copy-start.107 = (f32[1,1,1024]{2,0,1:T(1,128)S(1)}, f32[1,1,1024]{2,0,1:T(1,128)}, u32[]{:S(2)}) copy-start(f32[1,1,1024]{2,0,1:T(1,128)} %get-tuple-element.452) | copy-start | bytes 12292
  406.7 241.0 %copy-start.5 = (f32[1,520,1024]{2,1,0:T(8,128)}, f32[1,520,1024]{2,1,0:T(8,128)S(1)}, u32[]{:S(2)}) copy-start(f32[1,520,1024]{2,1,0:T(8,128)S(1)} %get-tuple-element.418) | copy-start | bytes 6389764
  406.7 95.2 %copy-start.58 = (f32[520]{0:T(1024)}, f32[520]{0:T(1024)S(1)}, u32[]{:S(2)}) copy-start(f32[520]{0:T(1024)S(1)} %broadcast_multiply_fusion.1) | copy-start | bytes 6244
  407.1 94.9 %copy-start.54 = (f32[520]{0:T(1024)}, f32[520]{0:T(1024)S(1)}, u32[]{:S(2)}) copy-start(f32[520]{0:T(1024)S(1)} %multiply_reduce_fusion.3) | copy-start | bytes 6244
  407.1 94.8 %copy-start.85 = (f32[520]{0:T(1024)}, f32[520]{0:T(1024)S(1)}, u32[]{:S(2)}) copy-start(f32[520]{0:T(1024)S(1)} %fusion.201) | copy-start | bytes 6244
  621.7 13.0 copy-start.38
  621.7 13.0 copy-start.40
  647.7 74.6 %copy-start.73 = (f32[1,4,1024]{2,0,1:T(1,128)S(1)}, f32[1,4,1024]{2,0,1:T(1,128)}, u32[]{:S(2)}) copy-start(f32[1,4,1024]{2,0,1:T(1,128)} %slice.281) | copy-start | bytes 49156
  647.7 74.6 %copy-start.74 = (f32[1,1,1024]{2,0,1:T(1,128)S(1)}, f32[1,1,1024]{2,0,1:T(1,128)}, u32[]{:S(2)}) copy-start(f32[1,1,1024]{2,0,1:T(1,128)} %get-tuple-element.447) | copy-start | bytes 12292
  647.7 74.5 %copy-start.101 = (f32[1,1,1024]{2,0,1:T(1,128)S(1)}, f32[1,1,1024]{2,0,1:T(1,128)}, u32[]{:S(2)}) copy-start(f32[1,1,1024]{2,0,1:T(1,128)} %get-tuple-element.448) | copy-start | bytes 12292
  652.5 122.1 %copy-start.61 = (f32[520]{0:T(1024)}, f32[520]{0:T(1024)S(1)}, u32[]{:S(2)}) copy-start(f32[520]{0:T(1024)S(1)} %broadcast_multiply_fusion) | copy-start | bytes 6244
  654.3 120.2 %copy-start.88 = (f32[520]{0:T(1024)}, f32[520]{0:T(1024)S(1)}, u32[]{:S(2)}) copy-start(f32[520]{0:T(1024)S(1)} %fusion.202) | copy-start | bytes 6244
  722.3 28.1 %copy-start.34 = (bf16[1,520,1024]{2,1,0:T(8,128)(2,1)S(1)}, bf16[1,520,1024]{2,1,0:T(8,128)(2,1)}, u32[]{:S(2)}) copy-start(bf16[1,520,1024]{2,1,0:T(8,128)(2,1)} %param.25) | copy-start | bytes 3194884
  722.3 28.1 %copy-start.78 = (f32[1,1,1024]{2,0,1:T(1,128)S(1)}, f32[1,1,1024]{2,0,1:T(1,128)}, u32[]{:S(2)}) copy-start(f32[1,1,1024]{2,0,1:T(1,128)} %get-tuple-element.445) | copy-start | bytes 12292
  750.4 14.6 copy-start.9
  937.0 14.4 copy-start.70
  952.4 14.3 copy-start.37
  952.4 14.3 copy-start.20
  952.4 14.3 copy-start.57
  952.4 14.3 copy-start.77
  952.4 14.3 copy-start.84
  966.7 10.0 copy-start.120
  1147.2 299.7 %reduce-scatter.13.cloned.1.call-start = ((), (), s32[]{:S(2)}) async-start(), calls=%async_computation.15 | async-start | bytes 9437184 | tf_op jit(solution)/shard_map/reduce_scatter | solution.py:292
  1167.7 564.7 %reduce-scatter.15.cloned.1.call-start = ((), (), s32[]{:S(2)}) async-start(), calls=%async_computation.16 | async-start | bytes 18874368 | tf_op jit(solution)/shard_map/reduce_scatter | solution.py:295
  1193.2 825.2 %reduce-scatter.17.cloned.1.call-start = ((), (), s32[]{:S(2)}) async-start(), calls=%async_computation.17 | async-start | bytes 18874368 | tf_op jit(solution)/shard_map/reduce_scatter | solution.py:295
  1219.4 863.3 %reduce-scatter.19.cloned.1.call-start = ((), (), s32[]{:S(2)}) async-start(), calls=%async_computation.24 | async-start | bytes 294912
  1233.9 912.9 %reduce-scatter.21.cloned.1.call-start = ((), (), s32[]{:S(2)}) async-start(), calls=%async_computation.25 | async-start | bytes 294912
  1237.5 781.0 %copy-start.13 = (f32[520,1024]{1,0:T(8,128)S(1)}, f32[520,1024]{1,0:T(8,128)}, u32[]{:S(2)}) copy-start(f32[520,1024]{1,0:T(8,128)} %copy-done.12) | copy-start | bytes 6389764
  1237.5 781.0 %copy-start.18 = (bf16[1,520,1024]{2,1,0:T(8,128)(2,1)S(1)}, bf16[1,520,1024]{2,1,0:T(8,128)(2,1)}, u32[]{:S(2)}) copy-start(bf16[1,520,1024]{2,1,0:T(8,128)(2,1)} %param.20) | copy-start | bytes 3194884
  1237.5 944.4 %all-gather.23.cloned.1.call-start = ((), (), s32[]{:S(2)}) async-start(), calls=%async_computation.22 | async-start | bytes 5242880 | tf_op jit(solution)/shard_map/all_gather | solution.py:303
  1294.4 923.4 %all-gather.25.cloned.1.call-start = ((), (), s32[]{:S(2)}) async-start(), calls=%async_computation.23 | async-start | bytes 5242880 | tf_op jit(solution)/shard_map/all_gather | solution.py:303
  1446.9 859.1 %all-reduce.4.cloned.1.call-start = ((), (), s32[]{:S(2)}) async-start(), calls=%async_computation.26 | async-start | bytes 8388608 | tf_op jit(solution)/shard_map/psum | solution.py:306
  2018.5 134.9 %copy-start.46 = (bf16[2,14,128]{2,0,1:T(2,128)(2,1)S(1)}, bf16[2,14,128]{2,0,1:T(2,128)(2,1)}, u32[]{:S(2)}) copy-start(bf16[2,14,128]{2,0,1:T(2,128)(2,1)} %param.24) | copy-start | bytes 21508
  2018.5 134.9 %copy-start.90 = (f32[2,14,128]{2,0,1:T(2,128)S(1)}, f32[2,14,128]{2,0,1:T(2,128)}, u32[]{:S(2)}) copy-start(f32[2,14,128]{2,0,1:T(2,128)} %param.30) | copy-start | bytes 43012
  2018.5 134.9 %copy-start.91 = (f32[2,14,128]{2,0,1:T(2,128)S(1)}, f32[2,14,128]{2,0,1:T(2,128)}, u32[]{:S(2)}) copy-start(f32[2,14,128]{2,0,1:T(2,128)} %param.31) | copy-start | bytes 43012
  2185.0 37.1 %copy-start.27 = (bf16[2,128,4096]{2,1,0:T(8,128)(2,1)S(1)}, bf16[2,128,4096]{2,1,0:T(8,128)(2,1)}, u32[]{:S(2)}) copy-start(bf16[2,128,4096]{2,1,0:T(8,128)(2,1)} %param.22) | copy-start | bytes 6291460
  (84 other events, 373.0 us)
Sparse Core Ops, SparseCore 0:
  10.7 128.7 all-gather.14
  142.2 225.7 all-gather.16
  370.8 123.1 all-gather.18
  496.5 225.7 all-gather.20
  1147.3 147.0 reduce-scatter.10
  1298.9 147.9 reduce-scatter.12
  1450.7 281.6 reduce-scatter.14
  1736.6 281.7 reduce-scatter.16
  2022.3 60.3 reduce-scatter.18
  2086.5 60.2 reduce-scatter.20
  2148.4 33.4 all-gather.22
  2183.3 34.4 all-gather.24
  2220.3 85.6 all-reduce.3
